TPU v7x, 32 devices: a whole 2x2x4 slice. The times are simulated.
32 devices in a mesh: pipe: 2 (over y), tensor: 4 (over z), dp: 4 (over x, core).
Axes of the slice: x: 2, y: 2, z: 4, core: 2. Of those that a mesh axis runs over, the one named last changes fastest.
Arguments:
- weights: bfloat16 [2, 4096, 4096], P('pipe', None, 'tensor'), may hold values from -0.09375 to 0.09375
- codes: int32 [2, 1024, 4096], P('pipe', 'dp'), may hold values from -127 to 127
- scales: float32 [2, 1024], P('pipe', 'dp'), may hold values from 0.004 to 0.04
- grad_out: bfloat16 [1024, 4096], P('dp', 'tensor'), may hold values from -6 to 6
Outputs:
- grad_in: bfloat16 [2, 1024, 4096], P('pipe', 'dp', 'tensor')
- weight_grad: float32 [2, 4096, 4096], P('pipe', 'dp', 'tensor')
Inputs may be any that keep to these rules, and one draw needn't show every extreme that they name: Symmetric integer codes of a per-token quantization.
All inputs are finite; a program needn't handle non-finite values.
Results may differ from a plain program's by a relative error of at most 0.028.
Values may be sent and summed in bfloat16 or wider, within the bound.
A program may use at most 64 MiB of HBM per device.

v0:
```python
import functools

import jax
import jax.numpy as jnp
from jax import lax
from jax.experimental import pallas as pl
from jax.experimental.pallas import tpu as pltpu
from jax.sharding import PartitionSpec as P

SIXTEENTHS = (4, 4, 4, 4)
STRIPS = 2
NT = (((1,), (1,)), ((), ()))


def relay_kernel(
    weights, codes, scales, grad_out,
    grad_in, g_all, x_all,
    w_buf, c_buf, s_buf, x_buf, g_buf, prod, from_left, from_right,
    w_sem, c_sem, g_sem, g_hop, hop_sem,
    right_send, right_recv, left_send, left_recv,
    g_send, g_recv, x_send, x_recv, g_own, x_own,
    *, sections, shards, replicas, pieces,
):
    section, shard, replica = (lax.axis_index(n) for n in ("pipe", "tensor", "dp"))
    is_last = section == sections - 1
    tok, cols = g_buf.shape
    micro = len(pieces)
    width = x_buf.shape[2]

    barrier = pltpu.get_barrier_semaphore()

    def greet(condition, target):
        @pl.when(condition)
        def _():
            pl.semaphore_signal(barrier, inc=1, device_id=target)

    def w_copy(j):
        part = pl.ds(pl.multiple_of(j * cols, cols), cols)
        return pltpu.make_async_copy(weights.at[part, :], w_buf.at[part, :], w_sem.at[j])

    def c_copy(o):
        peer = lax.rem(replica + o, replicas)
        part = pl.ds(pl.multiple_of(peer * width, width), width)
        return pltpu.make_async_copy(codes.at[:, part], c_buf.at[o], c_sem.at[o])

    def micro_rows(m):
        return pl.ds(*pieces[m])

    def head(ref, m, j):
        return ref.at[m, j, pl.ds(0, pieces[m][1]), :]

    def strip(m, h):
        size = pieces[m][1] // STRIPS
        return pl.ds(h * size, size)

    def strip_rows(m, h):
        size = pieces[m][1] // STRIPS
        return pl.ds(pieces[m][0] + h * size, size)

    def g_load(m):
        return pltpu.make_async_copy(grad_out.at[micro_rows(m), :], g_buf.at[micro_rows(m), :], g_sem.at[m])

    def order(i):
        return jnp.where(2 * shard < shards, shards - 1 - i, i)

    @pl.when(is_last)
    def _():
        for m in range(micro):
            g_load(m).start()

    @pl.loop(0, shards)
    def _(i):
        w_copy(order(i)).start()

    @pl.loop(0, replicas)
    def _(o):
        c_copy(o).start()

    greet(shard > 0, {"tensor": shard - 1})
    greet(shard < shards - 1, {"tensor": shard + 1})
    greet(section > 0, {"pipe": section - 1})
    greet(section < sections - 1, {"pipe": section + 1})

    @pl.loop(1, replicas)
    def _(o):
        pl.semaphore_signal(barrier, inc=1, device_id={"dp": lax.rem(replica + o, replicas)})

    def one(condition):
        return jnp.where(condition, 1, 0)

    pl.semaphore_wait(
        barrier,
        replicas - 1 + one(shard > 0) + one(shard < shards - 1) + one(section > 0) + one(section < sections - 1),
    )

    def hop(m, h):
        return pltpu.make_async_remote_copy(
            src_ref=grad_in.at[strip_rows(m, h), :], dst_ref=g_buf.at[strip_rows(m, h), :],
            send_sem=hop_sem.at[m * STRIPS + h], recv_sem=g_hop.at[m * STRIPS + h], device_id={"pipe": section - 1})

    def to_right(m, j, h):
        return pltpu.make_async_remote_copy(
            src_ref=prod.at[m, j, strip(m, h), :], dst_ref=from_left.at[m, j, strip(m, h), :],
            send_sem=right_send.at[m * STRIPS + h, j], recv_sem=right_recv.at[m * STRIPS + h, j], device_id={"tensor": shard + 1})

    def to_left(m, j, h):
        return pltpu.make_async_remote_copy(
            src_ref=prod.at[m, j, strip(m, h), :], dst_ref=from_right.at[m, j, strip(m, h), :],
            send_sem=left_send.at[m * STRIPS + h, j], recv_sem=left_recv.at[m * STRIPS + h, j], device_id={"tensor": shard - 1})

    def own_rows(source):
        return pl.ds(pl.multiple_of(source * tok, tok), tok)

    def g_share(m, o):
        landing = pl.ds(pl.multiple_of(replica * tok + pieces[m][0], 16), pieces[m][1])
        return pltpu.make_async_remote_copy(
            src_ref=g_buf.at[micro_rows(m), :], dst_ref=g_all.at[landing, :],
            send_sem=g_send.at[m, o], recv_sem=g_recv.at[m, o],
            device_id={"dp": lax.rem(replica + o, replicas)})

    def g_keep(m):
        landing = pl.ds(pl.multiple_of(replica * tok + pieces[m][0], 16), pieces[m][1])
        return pltpu.make_async_copy(g_buf.at[micro_rows(m), :], g_all.at[landing, :], g_own.at[m])

    def x_share(o):
        return pltpu.make_async_remote_copy(
            src_ref=x_buf.at[o], dst_ref=x_all.at[own_rows(replica), :],
            send_sem=x_send.at[o], recv_sem=x_recv.at[o],
            device_id={"dp": lax.rem(replica + o, replicas)})

    def x_keep():
        return pltpu.make_async_copy(x_buf.at[0], x_all.at[own_rows(replica), :], x_own)

    def dequantize():
        s_buf[...] = jnp.transpose(jnp.broadcast_to(scales[...], (128, tok)))

        @pl.loop(0, replicas)
        def _(i):
            o = replicas - 1 - i
            c_copy(o).wait()

            @pl.loop(0, 4)
            def _(m):
                part = pl.ds(pl.multiple_of(m * (tok // 4), tok // 4), tok // 4)
                value = c_buf[o, part, :].astype(jnp.float32) * s_buf[part, 0:1]
                x_buf[o, part, :] = value.astype(jnp.bfloat16)

            @pl.when(o > 0)
            def _():
                x_share(o).start()

        x_keep().start()

    def produce(m):
        @pl.when(is_last)
        def _():
            g_load(m).wait()

        @pl.when(jnp.logical_not(is_last))
        def _():
            for h in range(STRIPS):
                hop(m, h).wait_recv()

        @pl.loop(0, shards)
        def _(i):
            j = order(i)

            if m == 0:
                w_copy(j).wait()

            part = pl.ds(pl.multiple_of(j * cols, cols), cols)
            head(prod, m, j)[...] = lax.dot_general(
                g_buf[micro_rows(m), :], w_buf[part, :], NT, preferred_element_type=jnp.float32
            ).astype(jnp.bfloat16)

            @pl.when((shard == 0) & (j > 0))
            def _():
                for h in range(STRIPS):
                    to_right(m, j, h).start()

            @pl.when((shard == shards - 1) & (j < shards - 1))
            def _():
                for h in range(STRIPS):
                    to_left(m, j, h).start()

        g_keep(m).start()

        @pl.loop(1, replicas)
        def _(o):
            g_share(m, o).start()

    def add_in(m, j, h, arrived):
        part = strip(m, h)
        total = prod[m, j, part, :].astype(jnp.float32) + arrived[m, j, part, :].astype(jnp.float32)
        prod[m, j, part, :] = total.astype(jnp.bfloat16)

    def relay(m, rightward):
        @pl.loop(0, shards - 1)
        def _(i):
            far = shards - 1 - i

            @pl.when(rightward & (shard > 0) & (shard + far < shards))
            def _():
                j = shard + far
                for h in range(STRIPS):
                    to_right(m, j, h).wait_recv()
                    add_in(m, j, h, from_left)
                    to_right(m, j, h).start()

            @pl.when(jnp.logical_not(rightward) & (shard < shards - 1) & (shard - far >= 0))
            def _():
                j = shard - far
                for h in range(STRIPS):
                    to_left(m, j, h).wait_recv()
                    add_in(m, j, h, from_right)
                    to_left(m, j, h).start()

    def finish(m, h):
        part, inner = strip_rows(m, h), strip(m, h)

        @pl.when(shard > 0)
        def _():
            to_right(m, shard, h).wait_recv()

        @pl.when(shard < shards - 1)
        def _():
            to_left(m, shard, h).wait_recv()

        def of(ref):
            return ref[m, shard, inner, :].astype(jnp.float32)

        own = of(prod) + g_buf[part, :].astype(jnp.float32)

        @pl.when((shard > 0) & (shard < shards - 1))
        def _():
            grad_in[part, :] = (own + (of(from_left) + of(from_right))).astype(jnp.bfloat16)

        @pl.when(shard == 0)
        def _():
            grad_in[part, :] = (own + of(from_right)).astype(jnp.bfloat16)

        @pl.when(shard == shards - 1)
        def _():
            grad_in[part, :] = (own + of(from_left)).astype(jnp.bfloat16)

        @pl.when(section > 0)
        def _():
            hop(m, h).start()

    @pl.when(jnp.logical_not(is_last))
    def _():
        dequantize()

    near = 2 * shard < shards
    produce(0)

    @pl.when(is_last)
    def _():
        dequantize()

    for m in range(micro):
        relay(m, near)
        relay(m, jnp.logical_not(near))
        if m + 1 < micro:
            produce(m + 1)
        for h in range(STRIPS):
            finish(m, h)

    for m in range(micro):

        @pl.loop(0, shards)
        def _(j):
            @pl.when((j > shard))
            def _():
                for h in range(STRIPS):
                    to_right(m, j, h).wait_send()

            @pl.when((j < shard))
            def _():
                for h in range(STRIPS):
                    to_left(m, j, h).wait_send()

        @pl.when(section > 0)
        def _():
            for h in range(STRIPS):
                hop(m, h).wait_send()

        g_keep(m).wait()

        @pl.loop(1, replicas)
        def _(o):
            g_share(m, o).wait_send()
            g_share(m, o).wait_recv()

    x_keep().wait()

    @pl.loop(1, replicas)
    def _(o):
        x_share(o).wait_send()
        x_share(o).wait_recv()


def per_device(weights, codes, scales, grad_out):
    sections, shards, replicas = (lax.axis_size(n) for n in ("pipe", "tensor", "dp"))
    tok, cols = grad_out.shape
    depth = weights.shape[1]
    width = depth // replicas
    sizes = [tok * part // 16 for part in SIXTEENTHS]
    pieces = tuple((sum(sizes[:m]), size) for m, size in enumerate(sizes))
    micro, rows = len(sizes), max(sizes)
    strips = micro * STRIPS
    low = jnp.bfloat16
    dma = pltpu.SemaphoreType.DMA
    anywhere = pl.BlockSpec(memory_space=pl.ANY)
    far = pl.BlockSpec(memory_space=pltpu.MemorySpace.HBM)
    inside = pl.BlockSpec(memory_space=pltpu.VMEM)
    grad_in, g_all, x_all = pl.pallas_call(
        functools.partial(relay_kernel, sections=sections, shards=shards, replicas=replicas, pieces=pieces),
        out_shape=(
            jax.ShapeDtypeStruct((tok, cols), low),
            jax.ShapeDtypeStruct((replicas * tok, cols), low),
            jax.ShapeDtypeStruct((replicas * tok, width), low),
        ),
        in_specs=[far, far, inside, far],
        out_specs=(inside, anywhere, anywhere),
        scratch_shapes=[
            pltpu.VMEM((depth, cols), low),
            pltpu.VMEM((replicas, tok, width), jnp.int32),
            pltpu.VMEM((tok, 128), jnp.float32),
            pltpu.VMEM((replicas, tok, width), low),
            pltpu.VMEM((tok, cols), low),
            pltpu.VMEM((micro, shards, rows, cols), low),
            pltpu.VMEM((micro, shards, rows, cols), low),
            pltpu.VMEM((micro, shards, rows, cols), low),
            dma((shards,)), dma((replicas,)), dma((micro,)), dma((strips,)), dma((strips,)),
            dma((strips, shards)), dma((strips, shards)), dma((strips, shards)), dma((strips, shards)),
            dma((micro, replicas)), dma((micro, replicas)), dma((replicas,)), dma((replicas,)),
            dma((micro,)), dma(()),
        ],
        compiler_params=pltpu.CompilerParams(collective_id=0, has_side_effects=True, vmem_limit_bytes=48 * 2**20),
    )(weights[0], codes[0], scales, grad_out)
    weight_grad = lax.dot_general(x_all, g_all, (((0,), (0,)), ((), ())), preferred_element_type=jnp.float32)
    return grad_in[None], weight_grad[None]


def solution(mesh):
    placed = (P("pipe", None, "tensor"), P("pipe", "dp", None), P("pipe", "dp"), P("dp", "tensor"))
    return jax.shard_map(
        per_device,
        mesh=mesh,
        in_specs=placed,
        out_specs=(P("pipe", "dp", "tensor"), P("pipe", "dp", "tensor")),
        check_vma=False,
    )
```

profile of v0, /device:TPU:0, one launch (start us, length us, event | category | flops | bytes accessed | tf_op | source)
XLA Modules:
  0.0 69.9 jit_solution(11780648360539416426)
XLA Ops:
  0.6 0.0 copy-start
  0.6 1.0 %copy-done = bf16[256,1024]{1,0:T(8,128)(2,1)S(1)} copy-done((bf16[256,1024]{1,0:T(8,128)(2,1)S(1)}, bf16[256,1024]{1,0:T(8,128)(2,1)}, u32[]{:S(2)}) %copy-start) | copy-done | bytes 524312
  1.7 0.0 copy-start.1
  1.7 0.7 copy-done.1
  2.4 62.3 %shard_map.59 = (bf16[256,1024]{1,0:T(8,128)(2,1)S(1)}, bf16[1024,1024]{1,0:T(8,128)(2,1)S(1)}, bf16[1024,1024]{1,0:T(8,128)(2,1)S(1)}) custom-call(bf16[4096,1024]{1,0:T(8,128)(2,1)} %bitcast.8, s32[256,4096]{1,0:T(8,128)} %bitcast.9, f32[1,256]{1,0:T(1,128)S(1)} %copy-done.1, bf16[256,1024]{1,0:T(8,128)(2,1)S(1)} %copy-done), custom_call_target="tpu_custom_call" | custom-call | tf_op jit(solution)/shard_map/pallas_call | solution.py:317
  64.7 4.4 %convolution_bitcast_fusion = f32[1,1024,1024]{2,1,0:T(8,128)} fusion(bf16[1024,1024]{1,0:T(8,128)(2,1)S(1)} %get-tuple-element.6, bf16[1024,1024]{1,0:T(8,128)(2,1)S(1)} %get-tuple-element.7), kind=kOutput, calls=%fused_computation | convolution fusion | flops 2147483648 | bytes 8388608 | tf_op jit(solution)/shard_map/dot_general | solution.py:342
  69.1 0.8 %copy.7 = bf16[1,256,1024]{2,1,0:T(8,128)(2,1)} copy(bf16[1,256,1024]{2,1,0:T(8,128)(2,1)S(1)} %bitcast.7) | data formatting | bytes 1048576
Async XLA Ops:
  0.6 1.0 %copy-start = (bf16[256,1024]{1,0:T(8,128)(2,1)S(1)}, bf16[256,1024]{1,0:T(8,128)(2,1)}, u32[]{:S(2)}) copy-start(bf16[256,1024]{1,0:T(8,128)(2,1)} %grad_out.1) | copy-start | bytes 1572868
  1.7 0.7 copy-start.1
where the time goes:
time: 70.1 us; the launch traced here: 69.9 us
  Pallas kernels  62.3 us (89%)
  matrix products  4.45 us (6%)
  local copies, waits for them, and re-layouts  2.51 us (4%)
    pallas_call x1, Pallas kernels, per_device(): pl.pallas_call(functools.partial(relay_kernel, sections=sections, shards=...  62.3 us
    dot_general x1, matrix products, per_device(): lax.dot_general(x_all, g_all, (((0,), (0,)), ((), ())), preferred_element...  4.45 us
    unnamed x5, local copies, waits for them, and re-layouts  2.51 us

commit v1 on v0

v1 whole, which is shorter than its diff:
```python
import functools

import jax
import jax.numpy as jnp
from jax import lax
from jax.experimental import pallas as pl
from jax.experimental.pallas import tpu as pltpu
from jax.sharding import PartitionSpec as P

MICRO = 8
FAR_LAG, MID_LAG, END_LAG, PASS_LAG = 1, 3, 4, 4
LATE = 2
CODES_AT = 1
PROMPT, WAIT = 1, 1
NT = (((1,), (1,)), ((), ()))
TN = (((0,), (0,)), ((), ()))


def relay_kernel(
    weights, codes, scales, grad_out,
    grad_in, weight_grad,
    w_buf, c_buf, r_buf, s_buf, x_buf, x_all, g_all, prod, from_left, from_right, from_end,
    w_sem, c_sem, s_sem, g_sem, hop_send, hop_recv,
    sum_send, sum_recv, end_send, end_recv,
    g_send, g_recv, pass_send, pass_recv, x_send, x_recv,
    *, sections, shards, replicas,
):
    section, shard, replica = (lax.axis_index(n) for n in ("pipe", "tensor", "dp"))
    is_last = section == sections - 1
    tok, cols = grad_in.shape
    width = x_buf.shape[2]
    rows = tok // MICRO
    pairs = replicas // 2
    pair, side = replica // 2, lax.rem(replica, 2)
    sibling = 2 * pair + 1 - side
    at_left, at_right = shard == 0, shard == shards - 1
    at_end = at_left | at_right

    barrier = pltpu.get_barrier_semaphore()

    def greet(condition, target):
        @pl.when(condition)
        def _():
            pl.semaphore_signal(barrier, inc=1, device_id=target)

    def w_copy(j):
        part = pl.ds(pl.multiple_of(j * cols, cols), cols)
        return pltpu.make_async_copy(weights.at[part, :], w_buf.at[part, :], w_sem.at[j])

    def c_copy(o):
        peer = lax.rem(replica + o, replicas)
        part = pl.ds(pl.multiple_of(peer * width, width), width)
        return pltpu.make_async_copy(codes.at[:, part], c_buf.at[o], c_sem.at[o])

    def s_copy():
        return pltpu.make_async_copy(scales, r_buf, s_sem)

    def strip(m):
        return pl.ds(pl.multiple_of(m * rows, rows), rows)

    def held(source, m):
        return pl.ds(pl.multiple_of(source * tok + m * rows, rows), rows)

    def block(source):
        return pl.ds(pl.multiple_of(source * tok, tok), tok)

    def g_load():
        return pltpu.make_async_copy(grad_out, g_all.at[block(replica), :], g_sem)

    def order(i):
        step = jnp.where(at_end & (i < 2), 1 - i, i)
        return jnp.where(2 * shard < shards, shards - 1 - step, step)

    def load_codes():
        s_copy().start()

        @pl.loop(0, replicas)
        def _(i):
            c_copy(replicas - 1 - i).start()

    @pl.when(is_last)
    def _():
        g_load().start()

    @pl.when(jnp.logical_not(is_last))
    def _():
        load_codes()

    @pl.loop(0, shards)
    def _(i):
        w_copy(order(i)).start()

    greet(shard > 0, {"tensor": shard - 1})
    greet(shard < shards - 1, {"tensor": shard + 1})
    greet(at_end, {"tensor": shards - 1 - shard})
    greet(section > 0, {"pipe": section - 1})
    greet(section < sections - 1, {"pipe": section + 1})

    @pl.loop(1, replicas)
    def _(o):
        pl.semaphore_signal(barrier, inc=1, device_id={"dp": lax.rem(replica + o, replicas)})

    def one(condition):
        return jnp.where(condition, 1, 0)

    pl.semaphore_wait(
        barrier,
        replicas - 1 + one(shard > 0) + one(shard < shards - 1) + one(at_end) + one(section > 0) + one(section < sections - 1),
    )

    def hop(m):
        return pltpu.make_async_remote_copy(
            src_ref=grad_in.at[strip(m), :], dst_ref=g_all.at[held(replica, m), :],
            send_sem=hop_send, recv_sem=hop_recv.at[m], device_id={"pipe": section - 1})

    def to_right(m, j):
        return pltpu.make_async_remote_copy(
            src_ref=prod.at[j, strip(m), :], dst_ref=from_left.at[j, strip(m), :],
            send_sem=sum_send.at[j], recv_sem=sum_recv.at[m, j + 1], device_id={"tensor": shard + 1})

    def to_left(m, j):
        return pltpu.make_async_remote_copy(
            src_ref=prod.at[j, strip(m), :], dst_ref=from_right.at[j, strip(m), :],
            send_sem=sum_send.at[j], recv_sem=sum_recv.at[m, j], device_id={"tensor": shard - 1})

    def to_end(m):
        j = shards - 1 - shard
        return pltpu.make_async_remote_copy(
            src_ref=prod.at[j, strip(m), :], dst_ref=from_end.at[strip(m), :],
            send_sem=end_send, recv_sem=end_recv.at[m], device_id={"tensor": j})

    def g_share(m):
        return pltpu.make_async_remote_copy(
            src_ref=g_all.at[held(replica, m), :], dst_ref=g_all.at[held(replica, m), :],
            send_sem=g_send.at[0], recv_sem=g_recv.at[m, 0], device_id={"dp": sibling})

    def g_cross(m, o):
        return pltpu.make_async_remote_copy(
            src_ref=g_all.at[held(replica, m), :], dst_ref=g_all.at[held(replica, m), :],
            send_sem=g_send.at[o], recv_sem=g_recv.at[m, o],
            device_id={"dp": 2 * lax.rem(pair + o, pairs) + side})

    def g_pass(m, o):
        source = 2 * lax.rem(pair + pairs - o, pairs) + side
        return pltpu.make_async_remote_copy(
            src_ref=g_all.at[held(source, m), :], dst_ref=g_all.at[held(source, m), :],
            send_sem=pass_send.at[o], recv_sem=pass_recv.at[m, o], device_id={"dp": sibling})

    def x_share(o):
        return pltpu.make_async_remote_copy(
            src_ref=x_buf.at[o], dst_ref=x_all.at[block(replica), :],
            send_sem=x_send.at[o], recv_sem=x_recv.at[o],
            device_id={"dp": lax.rem(replica + o, replicas)})

    def dequantize():
        s_copy().wait()
        s_buf[...] = jnp.transpose(jnp.broadcast_to(r_buf[...], (128, tok)))

        @pl.loop(0, replicas)
        def _(i):
            o = replicas - 1 - i
            c_copy(o).wait()

            @pl.loop(0, 4)
            def _(m):
                part = pl.ds(pl.multiple_of(m * (tok // 4), tok // 4), tok // 4)
                own = pl.ds(pl.multiple_of(replica * tok + m * (tok // 4), tok // 4), tok // 4)
                value = (c_buf[o, part, :].astype(jnp.float32) * s_buf[part, 0:1]).astype(jnp.bfloat16)

                @pl.when(o > 0)
                def _():
                    x_buf[o, part, :] = value

                @pl.when(o == 0)
                def _():
                    x_all[own, :] = value

            @pl.when(o > 0)
            def _():
                x_share(o).start()

    def launch(m, j):
        straight = j == shards - 1 - shard

        @pl.when(at_end & straight)
        def _():
            to_end(m).start()

        @pl.when(at_left & (j > 0) & jnp.logical_not(straight))
        def _():
            to_right(m, j).start()

        @pl.when(at_right & (j < shards - 1) & jnp.logical_not(straight))
        def _():
            to_left(m, j).start()

    def launch_next(m):
        @pl.when(shard == 1)
        def _():
            to_right(m, shards - 1).start()

        @pl.when(shard == shards - 2)
        def _():
            to_left(m, 0).start()

    def spread(m):
        g_share(m).start()

        @pl.loop(1, pairs)
        def _(o):
            g_cross(m, o).start()

    def pass_on(m):
        @pl.loop(1, pairs)
        def _(o):
            g_cross(m, o).wait_recv()
            g_pass(m, o).start()

    def w_part(j):
        return w_buf[pl.ds(pl.multiple_of(j * cols, cols), cols), :]

    def produce_all():
        g_load().wait()

        @pl.loop(0, shards)
        def _(i):
            j = order(i)
            w_copy(j).wait()
            prod[j, :, :] = lax.dot_general(
                g_all[block(replica), :], w_part(j), NT, preferred_element_type=jnp.float32
            ).astype(jnp.bfloat16)
            launch(0, j)

            @pl.when(i == 0)
            def _():
                launch_next(0)

        @pl.loop(1, MICRO)
        def _(m):
            @pl.loop(0, shards)
            def _(i):
                launch(m, order(i))

        load_codes()

        @pl.loop(0, MICRO)
        def _(m):
            spread(m)

    def produce(m):
        hop(m).wait_recv()
        spread(m)

        @pl.loop(0, shards)
        def _(i):
            j = order(i)
            prod[j, strip(m), :] = lax.dot_general(
                g_all[held(replica, m), :], w_part(j), NT, preferred_element_type=jnp.float32
            ).astype(jnp.bfloat16)
            launch(m, j)

            @pl.when(i == 0)
            def _():
                launch_next(m)

    def add_in(m, j, arrived):
        part = strip(m)
        total = prod[j, part, :].astype(jnp.float32) + arrived[j, part, :].astype(jnp.float32)
        prod[j, part, :] = total.astype(jnp.bfloat16)

    def relay(m, rightward):
        @pl.loop(0, shards - 1)
        def _(i):
            far = shards - 1 - i
            right, left = shard + far, shard - far

            @pl.when(rightward & (shard > 0) & (right < shards) & ((shard > 1) | (right < shards - 1)))
            def _():
                to_right(m, right).wait_recv()
                add_in(m, right, from_left)
                to_right(m, right).start()

            @pl.when(jnp.logical_not(rightward) & (shard < shards - 1) & (left >= 0) & ((shard < shards - 2) | (left > 0)))
            def _():
                to_left(m, left).wait_recv()
                add_in(m, left, from_right)
                to_left(m, left).start()

    def finish(m):
        part = strip(m)

        @pl.when(shard > 0)
        def _():
            to_right(m, shard).wait_recv()

        @pl.when(shard < shards - 1)
        def _():
            to_left(m, shard).wait_recv()

        @pl.when(at_end)
        def _():
            to_end(m).wait_recv()

        def of(ref):
            return ref[shard, part, :].astype(jnp.float32)

        own = of(prod) + g_all[held(replica, m), :].astype(jnp.float32)

        @pl.when(jnp.logical_not(at_end))
        def _():
            grad_in[part, :] = (own + (of(from_left) + of(from_right))).astype(jnp.bfloat16)

        def settle(condition, inner):
            @pl.when(condition)
            def _():
                grad_in[part, :] = (own + (of(inner) + from_end[part, :].astype(jnp.float32))).astype(jnp.bfloat16)

        settle(at_left, from_right)
        settle(at_right, from_left)

        @pl.when(section > 0)
        def _():
            hop(m).start()

    near = 2 * shard < shards

    def relays(m):
        relay(m, near)
        relay(m, jnp.logical_not(near))

    @pl.when(is_last)
    def _():
        produce_all()

        @pl.loop(0, MICRO)
        def _(m):
            @pl.when(m + 1 < MICRO)
            def _():
                launch_next(m + 1)

            @pl.when(at_end)
            def _():
                finish(m)

            @pl.when(jnp.logical_not(at_end))
            def _():
                relays(m)

                @pl.when(m < PROMPT)
                def _():
                    finish(m)

                @pl.when(m >= PROMPT + WAIT)
                def _():
                    finish(m - WAIT)

            @pl.when(m == CODES_AT)
            def _():
                dequantize()

        @pl.when(jnp.logical_not(at_end))
        def _():
            @pl.loop(MICRO - WAIT, MICRO)
            def _(m):
                finish(m)

        @pl.loop(0, MICRO)
        def _(m):
            pass_on(m)

    @pl.when(jnp.logical_not(is_last))
    def _():
        dequantize()

        @pl.loop(0, shards)
        def _(i):
            w_copy(order(i)).wait()

        behind = jnp.where(at_end, END_LAG, MID_LAG)

        @pl.loop(0, MICRO)
        def _(s):
            def at(lag, action):
                @pl.when(s >= lag)
                def _():
                    action(s - lag)

            produce(s)
            at(FAR_LAG, lambda m: relay(m, jnp.logical_not(near)))
            at(PASS_LAG, pass_on)
            at(behind, finish)
            relay(s, near)

        @pl.loop(MICRO - FAR_LAG, MICRO)
        def _(m):
            relay(m, jnp.logical_not(near))

        @pl.loop(MICRO - PASS_LAG, MICRO)
        def _(m):
            pass_on(m)

        @pl.loop(MICRO - behind, MICRO - LATE)
        def _(m):
            finish(m)

    @pl.loop(1, replicas)
    def _(o):
        x_share(o).wait_recv()

    @pl.loop(0, MICRO)
    def _(m):
        g_share(m).wait_recv()

        @pl.loop(1, pairs)
        def _(o):
            g_pass(m, o).wait_recv()

    chunk = min(width, 256)

    @pl.loop(0, width // chunk)
    def _(i):
        part = pl.ds(pl.multiple_of(i * chunk, chunk), chunk)
        weight_grad[part, :] = lax.dot_general(x_all[:, part], g_all[...], TN, preferred_element_type=jnp.float32)

    @pl.when(jnp.logical_not(is_last))
    def _():
        @pl.loop(MICRO - LATE, MICRO)
        def _(m):
            finish(m)

    def sent(source, sem):
        pltpu.make_async_copy(source, source, sem).wait()

    @pl.loop(0, shards)
    def _(j):
        @pl.when((j != shard) & jnp.logical_not(at_end & (j == shards - 1 - shard)))
        def _():
            sent(prod.at[j], sum_send.at[j])

    @pl.when(at_end)
    def _():
        sent(prod.at[shards - 1 - shard], end_send)

    @pl.when(section > 0)
    def _():
        sent(grad_in, hop_send)

    sent(g_all.at[block(replica), :], g_send.at[0])

    @pl.loop(1, pairs)
    def _(o):
        sent(g_all.at[block(replica), :], g_send.at[o])
        sent(g_all.at[block(replica), :], pass_send.at[o])

    @pl.loop(1, replicas)
    def _(o):
        x_share(o).wait_send()


def per_device(weights, codes, scales, grad_out):
    sections, shards, replicas = (lax.axis_size(n) for n in ("pipe", "tensor", "dp"))
    tok, cols = grad_out.shape
    depth = weights.shape[1]
    width = depth // replicas
    pairs = replicas // 2
    low = jnp.bfloat16
    dma = pltpu.SemaphoreType.DMA
    far = pl.BlockSpec(memory_space=pltpu.MemorySpace.HBM)
    inside = pl.BlockSpec(memory_space=pltpu.VMEM)
    grad_in, weight_grad = pl.pallas_call(
        functools.partial(relay_kernel, sections=sections, shards=shards, replicas=replicas),
        out_shape=(
            pltpu.VMEM((tok, cols), low),
            pltpu.VMEM((width, cols), jnp.float32),
        ),
        in_specs=[far, far, far, far],
        out_specs=(inside, inside),
        scratch_shapes=[
            pltpu.VMEM((depth, cols), low),
            pltpu.VMEM((replicas, tok, width), jnp.int32),
            pltpu.VMEM((1, tok), jnp.float32),
            pltpu.VMEM((tok, 128), jnp.float32),
            pltpu.VMEM((replicas, tok, width), low),
            pltpu.VMEM((replicas * tok, width), low),
            pltpu.VMEM((replicas * tok, cols), low),
            pltpu.VMEM((shards, tok, cols), low),
            pltpu.VMEM((shards, tok, cols), low),
            pltpu.VMEM((shards, tok, cols), low),
            pltpu.VMEM((tok, cols), low),
            dma((shards,)), dma((replicas,)), dma(()), dma(()), dma(()), dma((MICRO,)),
            dma((shards,)), dma((MICRO, shards + 1)), dma(()), dma((MICRO,)),
            dma((pairs,)), dma((MICRO, pairs)), dma((pairs,)), dma((MICRO, pairs)),
            dma((replicas,)), dma((replicas,)),
        ],
        compiler_params=pltpu.CompilerParams(collective_id=0, has_side_effects=True, vmem_limit_bytes=58 * 2**20),
    )(weights[0], codes[0], scales, grad_out)
    return grad_in[None], weight_grad[None]


def solution(mesh):
    placed = (P("pipe", None, "tensor"), P("pipe", "dp", None), P("pipe", "dp"), P("dp", "tensor"))
    return jax.shard_map(
        per_device,
        mesh=mesh,
        in_specs=placed,
        out_specs=(P("pipe", "dp", "tensor"), P("pipe", "dp", "tensor")),
        check_vma=False,
    )
```

time: 70.1 us -> 63.1 us (0.900)
  matrix products: 4.45 us -> 0 us
  Pallas kernels: 62.3 us -> 59.5 us
    dot_general x1 -> x0, matrix products: 4.45 us -> none  [per_device(): lax.dot_general(x_all, g_all, (((0,), (0,)), ((), ())), preferred_element...]
    pallas_call x1, Pallas kernels: 62.3 us -> 59.5 us  [per_device(): pl.pallas_call(functools.partial(relay_kernel, sections=sections, shards=...]
    unnamed x5 -> x2, local copies, waits for them, and re-layouts: 2.51 us -> 2.81 us
where the time goes in v1:
time: 63.1 us; the launch traced here: 62.9 us
  Pallas kernels  59.5 us (94%)
  local copies, waits for them, and re-layouts  2.81 us (4%)
  between operations  0.64 us (1%)
    pallas_call x1, Pallas kernels, per_device(): pl.pallas_call(functools.partial(relay_kernel, sections=sections, shards=...  59.5 us
    unnamed x2, local copies, waits for them, and re-layouts  2.81 us

profile of v1, /device:TPU:0, one launch (start us, length us, event | category | flops | bytes accessed | tf_op | source)
XLA Modules:
  0.0 62.9 jit_solution(8113255038344671641)
XLA Ops:
  0.6 59.5 %shard_map.59 = (bf16[256,1024]{1,0:T(8,128)(2,1)S(1)}, f32[1024,1024]{1,0:T(8,128)S(1)}) custom-call(bf16[4096,1024]{1,0:T(8,128)(2,1)} %bitcast.6, s32[256,4096]{1,0:T(8,128)} %bitcast.7, f32[1,256]{1,0:T(1,128)} %scales.1, bf16[256,1024]{1,0:T(8,128)(2,1)} %grad_out.1), custom_call_target="tpu_custom_call" | custom-call | tf_op jit(solution)/shard_map/pallas_call | solution.py:470
  60.1 0.8 %copy.8 = bf16[1,256,1024]{2,1,0:T(8,128)(2,1)} copy(bf16[1,256,1024]{2,1,0:T(8,128)(2,1)S(1)} %bitcast.5) | data formatting | bytes 1048576
  60.9 2.0 %copy.9 = f32[1,1024,1024]{2,1,0:T(8,128)} copy(f32[1,1024,1024]{2,1,0:T(8,128)S(1)} %bitcast.4) | data formatting | bytes 8388608

commit v2 on v1

--- a/solution.py
+++ b/solution.py
@@ -12,6 +12,9 @@
 LATE = 2
 CODES_AT = 1
 PROMPT, WAIT = 1, 1
+FILL, FULL = 2, 6
+DRAIN, STOP = 4, 8
+LEAD = 2
 NT = (((1,), (1,)), ((), ()))
 TN = (((0,), (0,)), ((), ()))
 
@@ -19,9 +22,9 @@
 def relay_kernel(
     weights, codes, scales, grad_out,
     grad_in, weight_grad,
-    w_buf, c_buf, r_buf, s_buf, x_buf, x_all, g_all, prod, from_left, from_right, from_end,
+    w_buf, c_buf, r_buf, s_buf, x_buf, x_all, g_all, prod, from_left, from_right, from_end, stage,
     w_sem, c_sem, s_sem, g_sem, hop_send, hop_recv,
-    sum_send, sum_recv, end_send, end_recv,
+    sum_send, sum_recv, end_send, end_recv, stage_recv, carry_send,
     g_send, g_recv, pass_send, pass_recv, x_send, x_recv,
     *, sections, shards, replicas,
 ):
@@ -93,6 +96,8 @@
     greet(shard > 0, {"tensor": shard - 1})
     greet(shard < shards - 1, {"tensor": shard + 1})
     greet(at_end, {"tensor": shards - 1 - shard})
+    greet(at_end & (section > 0), {"pipe": section - 1, "tensor": shards - 1 - shard})
+    greet(at_end & (section < sections - 1), {"pipe": section + 1, "tensor": shards - 1 - shard})
     greet(section > 0, {"pipe": section - 1})
     greet(section < sections - 1, {"pipe": section + 1})
 
@@ -105,7 +110,8 @@
 
     pl.semaphore_wait(
         barrier,
-        replicas - 1 + one(shard > 0) + one(shard < shards - 1) + one(at_end) + one(section > 0) + one(section < sections - 1),
+        replicas - 1 + one(shard > 0) + one(shard < shards - 1) + one(at_end) + one(section > 0)
+        + one(section < sections - 1) + one(at_end & (section > 0)) + one(at_end & (section < sections - 1)),
     )
 
     def hop(m):
@@ -128,6 +134,26 @@
         return pltpu.make_async_remote_copy(
             src_ref=prod.at[j, strip(m), :], dst_ref=from_end.at[strip(m), :],
             send_sem=end_send, recv_sem=end_recv.at[m], device_id={"tensor": j})
+
+    def detoured(m):
+        return jnp.where(is_last, (m >= FILL) & (m < FULL), (m >= DRAIN) & (m < STOP))
+
+    def to_stage(m, k):
+        return pltpu.make_async_remote_copy(
+            src_ref=prod.at[shards - 1 - shard, strip(m), :], dst_ref=stage.at[k, strip(m), :],
+            send_sem=end_send, recv_sem=stage_recv.at[k, m], device_id={"pipe": section + (2 * k - 1)})
+
+    def carry(m, k):
+        to_stage(m, k).wait_recv()
+        pltpu.make_async_remote_copy(
+            src_ref=stage.at[k, strip(m), :], dst_ref=from_end.at[strip(m), :],
+            send_sem=carry_send.at[k], recv_sem=end_recv.at[m],
+            device_id={"pipe": section + (1 - 2 * k), "tensor": shards - 1 - shard}).start()
+
+    def carry_all(start, stop, k):
+        @pl.loop(start, stop)
+        def _(m):
+            carry(m, k)
 
     def g_share(m):
         return pltpu.make_async_remote_copy(
@@ -182,9 +208,17 @@
     def launch(m, j):
         straight = j == shards - 1 - shard
 
-        @pl.when(at_end & straight)
+        @pl.when(at_end & straight & jnp.logical_not(detoured(m)))
         def _():
             to_end(m).start()
+
+        @pl.when(at_end & straight & detoured(m) & is_last)
+        def _():
+            to_stage(m, 0).start()
+
+        @pl.when(at_end & straight & detoured(m) & jnp.logical_not(is_last))
+        def _():
+            to_stage(m, 1).start()
 
         @pl.when(at_left & (j > 0) & jnp.logical_not(straight))
         def _():
@@ -233,7 +267,9 @@
 
             @pl.when(i == 0)
             def _():
-                launch_next(0)
+                @pl.loop(0, LEAD)
+                def _(m):
+                    launch_next(m)
 
         @pl.loop(1, MICRO)
         def _(m):
@@ -334,10 +370,6 @@
 
         @pl.loop(0, MICRO)
         def _(m):
-            @pl.when(m + 1 < MICRO)
-            def _():
-                launch_next(m + 1)
-
             @pl.when(at_end)
             def _():
                 finish(m)
@@ -345,6 +377,10 @@
             @pl.when(jnp.logical_not(at_end))
             def _():
                 relays(m)
+
+                @pl.when(m + LEAD < MICRO)
+                def _():
+                    launch_next(m + LEAD)
 
                 @pl.when(m < PROMPT)
                 def _():
@@ -368,9 +404,15 @@
         def _(m):
             pass_on(m)
 
+    below, above = at_end & (section > 0), at_end & (section == sections - 2)
+
     @pl.when(jnp.logical_not(is_last))
     def _():
         dequantize()
+
+        @pl.when(above)
+        def _():
+            carry_all(FILL, FULL, 0)
 
         @pl.loop(0, shards)
         def _(i):
@@ -403,6 +445,10 @@
         def _(m):
             finish(m)
 
+    @pl.when(below)
+    def _():
+        carry_all(DRAIN, STOP, 1)
+
     @pl.loop(1, replicas)
     def _(o):
         x_share(o).wait_recv()
@@ -440,6 +486,14 @@
     @pl.when(at_end)
     def _():
         sent(prod.at[shards - 1 - shard], end_send)
+
+    @pl.when(above)
+    def _():
+        sent(stage.at[0, pl.ds(0, (FULL - FILL) * rows), :], carry_send.at[0])
+
+    @pl.when(below)
+    def _():
+        sent(stage.at[1, pl.ds(0, (STOP - DRAIN) * rows), :], carry_send.at[1])
 
     @pl.when(section > 0)
     def _():
@@ -487,8 +541,9 @@
             pltpu.VMEM((shards, tok, cols), low),
             pltpu.VMEM((shards, tok, cols), low),
             pltpu.VMEM((tok, cols), low),
+            pltpu.VMEM((2, tok, cols), low),
             dma((shards,)), dma((replicas,)), dma(()), dma(()), dma(()), dma((MICRO,)),
-            dma((shards,)), dma((MICRO, shards + 1)), dma(()), dma((MICRO,)),
+            dma((shards,)), dma((MICRO, shards + 1)), dma(()), dma((MICRO,)), dma((2, MICRO)), dma((2,)),
             dma((pairs,)), dma((MICRO, pairs)), dma((pairs,)), dma((MICRO, pairs)),
             dma((replicas,)), dma((replicas,)),
         ],

time: 63.1 us -> 58.2 us (0.922)
  Pallas kernels: 59.5 us -> 54.6 us
    pallas_call x1, Pallas kernels: 59.5 us -> 54.6 us  [per_device(): pl.pallas_call(functools.partial(relay_kernel, sections=sections, shards=...]
where the time goes in v2:
time: 58.2 us; the launch traced here: 58.1 us
  Pallas kernels  54.6 us (94%)
  local copies, waits for them, and re-layouts  2.81 us (5%)
  between operations  0.64 us (1%)
    pallas_call x1, Pallas kernels, per_device(): pl.pallas_call(functools.partial(relay_kernel, sections=sections, shards=...  54.6 us
    unnamed x2, local copies, waits for them, and re-layouts  2.81 us

profile of v2, /device:TPU:0, one launch (start us, length us, event | category | flops | bytes accessed | tf_op | source)
XLA Modules:
  0.0 58.1 jit_solution(13642974488533961223)
XLA Ops:
  0.6 54.6 %shard_map.59 = (bf16[256,1024]{1,0:T(8,128)(2,1)S(1)}, f32[1024,1024]{1,0:T(8,128)S(1)}) custom-call(bf16[4096,1024]{1,0:T(8,128)(2,1)} %bitcast.6, s32[256,4096]{1,0:T(8,128)} %bitcast.7, f32[1,256]{1,0:T(1,128)} %scales.1, bf16[256,1024]{1,0:T(8,128)(2,1)} %grad_out.1), custom_call_target="tpu_custom_call" | custom-call | tf_op jit(solution)/shard_map/pallas_call | solution.py:524
  55.3 0.8 %copy.8 = bf16[1,256,1024]{2,1,0:T(8,128)(2,1)} copy(bf16[1,256,1024]{2,1,0:T(8,128)(2,1)S(1)} %bitcast.5) | data formatting | bytes 1048576
  56.1 2.0 %copy.9 = f32[1,1024,1024]{2,1,0:T(8,128)} copy(f32[1,1024,1024]{2,1,0:T(8,128)S(1)} %bitcast.4) | data formatting | bytes 8388608

commit v3 on v2

--- a/solution.py
+++ b/solution.py
@@ -8,24 +8,48 @@
 from jax.sharding import PartitionSpec as P
 
 MICRO = 8
-FAR_LAG, MID_LAG, END_LAG, PASS_LAG = 1, 3, 4, 4
-LATE = 2
+NEAR_LAG, FAR_LAG, MID_LAG, END_LAG, PASS_LAG = 1, 1, 3, 4, 4
+MID_LATE, END_LATE = 3, 4
 CODES_AT = 1
 PROMPT, WAIT = 1, 1
-FILL, FULL = 2, 6
+FILL, FULL = 1, 5
 DRAIN, STOP = 4, 8
 LEAD = 2
+STEPS, KEPT = 4, 2
+LIMIT = 32
 NT = (((1,), (1,)), ((), ()))
 TN = (((0,), (0,)), ((), ()))
 
 
+def rows_a_step(width):
+    return max(width // STEPS, 128)
+
+
+def closing_kernel(grad, part, x_all, g_all, grad_in, weight_grad, held, sems, own_sem, part_sem):
+    done, width = part.shape[0], x_all.shape[1]
+    chunk = rows_a_step(width)
+    copies = [
+        pltpu.make_async_copy(part, weight_grad.at[pl.ds(0, done), :], part_sem),
+        pltpu.make_async_copy(grad, grad_in, own_sem),
+    ]
+    for copy in copies:
+        copy.start()
+    for i, start in enumerate(range(done, width, chunk)):
+        held[i, :, :] = lax.dot_general(
+            x_all[:, pl.ds(start, chunk)], g_all[...], TN, preferred_element_type=jnp.float32)
+        copies.append(pltpu.make_async_copy(held.at[i], weight_grad.at[pl.ds(start, chunk), :], sems.at[i]))
+        copies[-1].start()
+    for copy in copies:
+        copy.wait()
+
+
 def relay_kernel(
     weights, codes, scales, grad_out,
-    grad_in, weight_grad,
-    w_buf, c_buf, r_buf, s_buf, x_buf, x_all, g_all, prod, from_left, from_right, from_end, stage,
+    grad_in, weight_part, x_all, g_all,
+    w_buf, c_buf, r_buf, s_buf, x_buf, prod, from_left, from_right, from_end, stage,
     w_sem, c_sem, s_sem, g_sem, hop_send, hop_recv,
     sum_send, sum_recv, end_send, end_recv, stage_recv, carry_send,
-    g_send, g_recv, pass_send, pass_recv, x_send, x_recv,
+    g_send, share_recv, g_recv, pass_send, pass_recv, x_send, x_recv,
     *, sections, shards, replicas,
 ):
     section, shard, replica = (lax.axis_index(n) for n in ("pipe", "tensor", "dp"))
@@ -96,8 +120,6 @@
     greet(shard > 0, {"tensor": shard - 1})
     greet(shard < shards - 1, {"tensor": shard + 1})
     greet(at_end, {"tensor": shards - 1 - shard})
-    greet(at_end & (section > 0), {"pipe": section - 1, "tensor": shards - 1 - shard})
-    greet(at_end & (section < sections - 1), {"pipe": section + 1, "tensor": shards - 1 - shard})
     greet(section > 0, {"pipe": section - 1})
     greet(section < sections - 1, {"pipe": section + 1})
 
@@ -111,7 +133,7 @@
     pl.semaphore_wait(
         barrier,
         replicas - 1 + one(shard > 0) + one(shard < shards - 1) + one(at_end) + one(section > 0)
-        + one(section < sections - 1) + one(at_end & (section > 0)) + one(at_end & (section < sections - 1)),
+        + one(section < sections - 1),
     )
 
     def hop(m):
@@ -141,7 +163,7 @@
     def to_stage(m, k):
         return pltpu.make_async_remote_copy(
             src_ref=prod.at[shards - 1 - shard, strip(m), :], dst_ref=stage.at[k, strip(m), :],
-            send_sem=end_send, recv_sem=stage_recv.at[k, m], device_id={"pipe": section + (2 * k - 1)})
+            send_sem=end_send, recv_sem=stage_recv.at[k, m - (FILL, DRAIN)[k]], device_id={"pipe": section + (2 * k - 1)})
 
     def carry(m, k):
         to_stage(m, k).wait_recv()
@@ -158,19 +180,19 @@
     def g_share(m):
         return pltpu.make_async_remote_copy(
             src_ref=g_all.at[held(replica, m), :], dst_ref=g_all.at[held(replica, m), :],
-            send_sem=g_send.at[0], recv_sem=g_recv.at[m, 0], device_id={"dp": sibling})
+            send_sem=g_send.at[0], recv_sem=share_recv, device_id={"dp": sibling})
 
     def g_cross(m, o):
         return pltpu.make_async_remote_copy(
             src_ref=g_all.at[held(replica, m), :], dst_ref=g_all.at[held(replica, m), :],
-            send_sem=g_send.at[o], recv_sem=g_recv.at[m, o],
+            send_sem=g_send.at[o], recv_sem=g_recv.at[m, o - 1],
             device_id={"dp": 2 * lax.rem(pair + o, pairs) + side})
 
     def g_pass(m, o):
         source = 2 * lax.rem(pair + pairs - o, pairs) + side
         return pltpu.make_async_remote_copy(
             src_ref=g_all.at[held(source, m), :], dst_ref=g_all.at[held(source, m), :],
-            send_sem=pass_send.at[o], recv_sem=pass_recv.at[m, o], device_id={"dp": sibling})
+            send_sem=pass_send.at[o], recv_sem=pass_recv.at[o], device_id={"dp": sibling})
 
     def x_share(o):
         return pltpu.make_async_remote_copy(
@@ -271,17 +293,13 @@
                 def _(m):
                     launch_next(m)
 
-        @pl.loop(1, MICRO)
-        def _(m):
-            @pl.loop(0, shards)
-            def _(i):
-                launch(m, order(i))
-
-        load_codes()
-
-        @pl.loop(0, MICRO)
-        def _(m):
-            spread(m)
+        @pl.when(at_end)
+        def _():
+            @pl.loop(1, MICRO)
+            def _(m):
+                @pl.loop(0, shards)
+                def _(i):
+                    launch(m, order(i))
 
     def produce(m):
         hop(m).wait_recv()
@@ -359,6 +377,7 @@
             hop(m).start()
 
     near = 2 * shard < shards
+    late = jnp.where(at_end, END_LATE, MID_LATE)
 
     def relays(m):
         relay(m, near)
@@ -370,10 +389,6 @@
 
         @pl.loop(0, MICRO)
         def _(m):
-            @pl.when(at_end)
-            def _():
-                finish(m)
-
             @pl.when(jnp.logical_not(at_end))
             def _():
                 relays(m)
@@ -382,6 +397,20 @@
                 def _():
                     launch_next(m + LEAD)
 
+            @pl.when(m == 0)
+            def _():
+                load_codes()
+
+                @pl.loop(0, MICRO)
+                def _(n):
+                    spread(n)
+
+            @pl.when(at_end)
+            def _():
+                finish(m)
+
+            @pl.when(jnp.logical_not(at_end))
+            def _():
                 @pl.when(m < PROMPT)
                 def _():
                     finish(m)
@@ -428,10 +457,14 @@
                     action(s - lag)
 
             produce(s)
+            at(NEAR_LAG, lambda m: relay(m, near))
             at(FAR_LAG, lambda m: relay(m, jnp.logical_not(near)))
             at(PASS_LAG, pass_on)
             at(behind, finish)
-            relay(s, near)
+
+        @pl.loop(MICRO - NEAR_LAG, MICRO)
+        def _(m):
+            relay(m, near)
 
         @pl.loop(MICRO - FAR_LAG, MICRO)
         def _(m):
@@ -441,7 +474,7 @@
         def _(m):
             pass_on(m)
 
-        @pl.loop(MICRO - behind, MICRO - LATE)
+        @pl.loop(MICRO - behind, MICRO - late)
         def _(m):
             finish(m)
 
@@ -453,29 +486,27 @@
     def _(o):
         x_share(o).wait_recv()
 
-    @pl.loop(0, MICRO)
-    def _(m):
-        g_share(m).wait_recv()
-
-        @pl.loop(1, pairs)
-        def _(o):
-            g_pass(m, o).wait_recv()
-
-    chunk = min(width, 256)
-
-    @pl.loop(0, width // chunk)
+    def sent(source, sem):
+        pltpu.make_async_copy(source, source, sem).wait()
+
+    sent(g_all.at[block(sibling), :], share_recv)
+
+    @pl.loop(1, pairs)
+    def _(o):
+        sent(g_all.at[block(2 * lax.rem(pair + pairs - o, pairs) + 1 - side), :], pass_recv.at[o])
+
+    chunk = rows_a_step(width)
+
+    @pl.loop(0, weight_part.shape[0] // chunk)
     def _(i):
         part = pl.ds(pl.multiple_of(i * chunk, chunk), chunk)
-        weight_grad[part, :] = lax.dot_general(x_all[:, part], g_all[...], TN, preferred_element_type=jnp.float32)
+        weight_part[part, :] = lax.dot_general(x_all[:, part], g_all[...], TN, preferred_element_type=jnp.float32)
 
     @pl.when(jnp.logical_not(is_last))
     def _():
-        @pl.loop(MICRO - LATE, MICRO)
+        @pl.loop(MICRO - late, MICRO)
         def _(m):
             finish(m)
-
-    def sent(source, sem):
-        pltpu.make_async_copy(source, source, sem).wait()
 
     @pl.loop(0, shards)
     def _(j):
@@ -521,34 +552,48 @@
     dma = pltpu.SemaphoreType.DMA
     far = pl.BlockSpec(memory_space=pltpu.MemorySpace.HBM)
     inside = pl.BlockSpec(memory_space=pltpu.VMEM)
-    grad_in, weight_grad = pl.pallas_call(
+    chunk = rows_a_step(width)
+    done = min(KEPT, width // chunk - 1) * chunk
+    later = (width - done) // chunk
+    handed = pl.pallas_call(
         functools.partial(relay_kernel, sections=sections, shards=shards, replicas=replicas),
         out_shape=(
             pltpu.VMEM((tok, cols), low),
-            pltpu.VMEM((width, cols), jnp.float32),
+            pltpu.VMEM((done, cols), jnp.float32),
+            pltpu.VMEM((replicas * tok, width), low),
+            pltpu.VMEM((replicas * tok, cols), low),
         ),
         in_specs=[far, far, far, far],
-        out_specs=(inside, inside),
+        out_specs=(inside,) * 4,
         scratch_shapes=[
             pltpu.VMEM((depth, cols), low),
             pltpu.VMEM((replicas, tok, width), jnp.int32),
             pltpu.VMEM((1, tok), jnp.float32),
             pltpu.VMEM((tok, 128), jnp.float32),
             pltpu.VMEM((replicas, tok, width), low),
-            pltpu.VMEM((replicas * tok, width), low),
-            pltpu.VMEM((replicas * tok, cols), low),
             pltpu.VMEM((shards, tok, cols), low),
             pltpu.VMEM((shards, tok, cols), low),
             pltpu.VMEM((shards, tok, cols), low),
             pltpu.VMEM((tok, cols), low),
             pltpu.VMEM((2, tok, cols), low),
             dma((shards,)), dma((replicas,)), dma(()), dma(()), dma(()), dma((MICRO,)),
-            dma((shards,)), dma((MICRO, shards + 1)), dma(()), dma((MICRO,)), dma((2, MICRO)), dma((2,)),
-            dma((pairs,)), dma((MICRO, pairs)), dma((pairs,)), dma((MICRO, pairs)),
+            dma((shards,)), dma((MICRO, shards + 1)), dma(()), dma((MICRO,)), dma((2, max(FULL - FILL, STOP - DRAIN))), dma((2,)),
+            dma((pairs,)), dma(()), dma((MICRO, pairs - 1)), dma((pairs,)), dma((pairs,)),
             dma((replicas,)), dma((replicas,)),
         ],
-        compiler_params=pltpu.CompilerParams(collective_id=0, has_side_effects=True, vmem_limit_bytes=58 * 2**20),
+        compiler_params=pltpu.CompilerParams(collective_id=0, has_side_effects=True, vmem_limit_bytes=57 * 2**20),
     )(weights[0], codes[0], scales, grad_out)
+    grad_in, weight_grad = pl.pallas_call(
+        closing_kernel,
+        out_shape=(
+            jax.ShapeDtypeStruct((tok, cols), low),
+            jax.ShapeDtypeStruct((width, cols), jnp.float32),
+        ),
+        in_specs=[inside] * 4,
+        out_specs=(far, far),
+        scratch_shapes=[pltpu.VMEM((later, chunk, cols), jnp.float32), dma((later,)), dma(()), dma(())],
+        compiler_params=pltpu.CompilerParams(vmem_limit_bytes=LIMIT * 2**20),
+    )(*handed)
     return grad_in[None], weight_grad[None]
 
 

time: 58.2 us -> 55 us (0.945)
  local copies, waits for them, and re-layouts: 2.81 us -> 0 us
    unnamed x2 -> x0, local copies, waits for them, and re-layouts: 2.81 us -> none
    pallas_call x1, Pallas kernels: 54.6 us -> 51.9 us  [per_device(): pl.pallas_call(functools.partial(relay_kernel, sections=sections, shards=...]
    pallas_call x0 -> x1, Pallas kernels: none -> 2.3 us  [per_device(): pl.pallas_call(closing_kernel, out_shape=(jax.ShapeDtypeStruct((tok, cols...]
where the time goes in v3:
time: 55 us; the launch traced here: 54.8 us
  Pallas kernels  54.2 us (99%)
  between operations  0.64 us (1%)
    pallas_call x1, Pallas kernels, per_device(): pl.pallas_call(functools.partial(relay_kernel, sections=sections, shards=...  51.9 us
    pallas_call x1, Pallas kernels, per_device(): pl.pallas_call(closing_kernel, out_shape=(jax.ShapeDtypeStruct((tok, cols...  2.3 us

profile of v3, /device:TPU:0, one launch (start us, length us, event | category | flops | bytes accessed | tf_op | source)
XLA Modules:
  0.0 54.8 jit_solution(1102534997995796777)
XLA Ops:
  0.6 51.9 %shard_map.59 = (bf16[256,1024]{1,0:T(8,128)(2,1)S(1)}, f32[512,1024]{1,0:T(8,128)S(1)}, bf16[1024,1024]{1,0:T(8,128)(2,1)S(1)}, bf16[1024,1024]{1,0:T(8,128)(2,1)S(1)}) custom-call(bf16[4096,1024]{1,0:T(8,128)(2,1)} %bitcast.4, s32[256,4096]{1,0:T(8,128)} %bitcast.5, f32[1,256]{1,0:T(1,128)} %scales.1, bf16[256,1024]{1,0:T(8,128)(2,1)} %grad_out.1), custom_call_target="tpu_custom_call" | custom-call | tf_op jit(solution)/shard_map/pallas_call | solution.py:558
  52.5 2.3 %shard_map.60 = (bf16[256,1024]{1,0:T(8,128)(2,1)}, f32[1024,1024]{1,0:T(8,128)}) custom-call(bf16[256,1024]{1,0:T(8,128)(2,1)S(1)} %get-tuple-element.8.grad, f32[512,1024]{1,0:T(8,128)S(1)} %get-tuple-element.9.part, bf16[1024,1024]{1,0:T(8,128)(2,1)S(1)} %get-tuple-element.10.x_all, bf16[1024,1024]{1,0:T(8,128)(2,1)S(1)} %get-tuple-element.11.g_all), custom_call_target="tpu_custom_call" | custom-call | tf_op jit(solution)/shard_map/pallas_call | solution.py:586

commit v4 on v3

--- a/solution.py
+++ b/solution.py
@@ -94,8 +94,8 @@
     def g_load():
         return pltpu.make_async_copy(grad_out, g_all.at[block(replica), :], g_sem)
 
-    def order(i):
-        step = jnp.where(at_end & (i < 2), 1 - i, i)
+    def order(i, far_first=False):
+        step = jnp.where(at_end & (i < 2) & jnp.logical_not(far_first), 1 - i, i)
         return jnp.where(2 * shard < shards, shards - 1 - step, step)
 
     def load_codes():
@@ -307,7 +307,7 @@
 
         @pl.loop(0, shards)
         def _(i):
-            j = order(i)
+            j = order(i, detoured(m))
             prod[j, strip(m), :] = lax.dot_general(
                 g_all[held(replica, m), :], w_part(j), NT, preferred_element_type=jnp.float32
             ).astype(jnp.bfloat16)

time: 55 us -> 54.7 us (level)
  no operation moved by 1% of the time
where the time goes in v4:
time: 54.7 us; the launch traced here: 54.5 us
  Pallas kernels  53.9 us (99%)
  between operations  0.64 us (1%)
    pallas_call x1, Pallas kernels, per_device(): pl.pallas_call(functools.partial(relay_kernel, sections=sections, shards=...  51.6 us
    pallas_call x1, Pallas kernels, per_device(): pl.pallas_call(closing_kernel, out_shape=(jax.ShapeDtypeStruct((tok, cols...  2.3 us

profile of v4, /device:TPU:0, one launch (start us, length us, event | category | flops | bytes accessed | tf_op | source)
XLA Modules:
  0.0 54.5 jit_solution(17553543162899292316)
XLA Ops:
  0.6 51.6 %shard_map.59 = (bf16[256,1024]{1,0:T(8,128)(2,1)S(1)}, f32[512,1024]{1,0:T(8,128)S(1)}, bf16[1024,1024]{1,0:T(8,128)(2,1)S(1)}, bf16[1024,1024]{1,0:T(8,128)(2,1)S(1)}) custom-call(bf16[4096,1024]{1,0:T(8,128)(2,1)} %bitcast.4, s32[256,4096]{1,0:T(8,128)} %bitcast.5, f32[1,256]{1,0:T(1,128)} %scales.1, bf16[256,1024]{1,0:T(8,128)(2,1)} %grad_out.1), custom_call_target="tpu_custom_call" | custom-call | tf_op jit(solution)/shard_map/pallas_call | solution.py:558
  52.2 2.3 %shard_map.60 = (bf16[256,1024]{1,0:T(8,128)(2,1)}, f32[1024,1024]{1,0:T(8,128)}) custom-call(bf16[256,1024]{1,0:T(8,128)(2,1)S(1)} %get-tuple-element.8.grad, f32[512,1024]{1,0:T(8,128)S(1)} %get-tuple-element.9.part, bf16[1024,1024]{1,0:T(8,128)(2,1)S(1)} %get-tuple-element.10.x_all, bf16[1024,1024]{1,0:T(8,128)(2,1)S(1)} %get-tuple-element.11.g_all), custom_call_target="tpu_custom_call" | custom-call | tf_op jit(solution)/shard_map/pallas_call | solution.py:586

commit v5 on v4

--- a/solution.py
+++ b/solution.py
@@ -17,6 +17,7 @@
 LEAD = 2
 STEPS, KEPT = 4, 2
 LIMIT = 32
+FAR_AT = 2
 NT = (((1,), (1,)), ((), ()))
 TN = (((0,), (0,)), ((), ()))
 
@@ -62,6 +63,8 @@
     sibling = 2 * pair + 1 - side
     at_left, at_right = shard == 0, shard == shards - 1
     at_end = at_left | at_right
+    near = 2 * shard < shards
+    one_step = shards <= 4
 
     barrier = pltpu.get_barrier_semaphore()
 
@@ -317,6 +320,11 @@
             def _():
                 launch_next(m)
 
+            if one_step:
+                @pl.when((i == FAR_AT) & (m >= FAR_LAG))
+                def _():
+                    relay(m - FAR_LAG, jnp.logical_not(near))
+
     def add_in(m, j, arrived):
         part = strip(m)
         total = prod[j, part, :].astype(jnp.float32) + arrived[j, part, :].astype(jnp.float32)
@@ -376,7 +384,6 @@
         def _():
             hop(m).start()
 
-    near = 2 * shard < shards
     late = jnp.where(at_end, END_LATE, MID_LATE)
 
     def relays(m):
@@ -458,17 +465,15 @@
 
             produce(s)
             at(NEAR_LAG, lambda m: relay(m, near))
-            at(FAR_LAG, lambda m: relay(m, jnp.logical_not(near)))
+            if not one_step:
+                at(FAR_LAG, lambda m: relay(m, jnp.logical_not(near)))
             at(PASS_LAG, pass_on)
             at(behind, finish)
 
-        @pl.loop(MICRO - NEAR_LAG, MICRO)
-        def _(m):
-            relay(m, near)
-
-        @pl.loop(MICRO - FAR_LAG, MICRO)
-        def _(m):
-            relay(m, jnp.logical_not(near))
+        for rightward in (jnp.logical_not(near), near) if one_step else (near, jnp.logical_not(near)):
+            @pl.loop(MICRO - 1, MICRO)
+            def _(m):
+                relay(m, rightward)
 
         @pl.loop(MICRO - PASS_LAG, MICRO)
         def _(m):

time: 54.7 us -> 56.3 us (1.029)
  Pallas kernels: 53.9 us -> 55.5 us
    pallas_call x1, Pallas kernels: 51.6 us -> 53.2 us  [per_device(): pl.pallas_call(functools.partial(relay_kernel, sections=sections, shards=...]
where the time goes in v5:
time: 56.3 us; the launch traced here: 56.2 us
  Pallas kernels  55.5 us (99%)
  between operations  0.64 us (1%)
    pallas_call x1, Pallas kernels, per_device(): pl.pallas_call(functools.partial(relay_kernel, sections=sections, shards=...  53.2 us
    pallas_call x1, Pallas kernels, per_device(): pl.pallas_call(closing_kernel, out_shape=(jax.ShapeDtypeStruct((tok, cols...  2.3 us

profile of v5, /device:TPU:0, one launch (start us, length us, event | category | flops | bytes accessed | tf_op | source)
XLA Modules:
  0.0 56.2 jit_solution(15812790375846131834)
XLA Ops:
  0.6 53.2 %shard_map.59 = (bf16[256,1024]{1,0:T(8,128)(2,1)S(1)}, f32[512,1024]{1,0:T(8,128)S(1)}, bf16[1024,1024]{1,0:T(8,128)(2,1)S(1)}, bf16[1024,1024]{1,0:T(8,128)(2,1)S(1)}) custom-call(bf16[4096,1024]{1,0:T(8,128)(2,1)} %bitcast.4, s32[256,4096]{1,0:T(8,128)} %bitcast.5, f32[1,256]{1,0:T(1,128)} %scales.1, bf16[256,1024]{1,0:T(8,128)(2,1)} %grad_out.1), custom_call_target="tpu_custom_call" | custom-call | tf_op jit(solution)/shard_map/pallas_call | solution.py:563
  53.9 2.3 %shard_map.60 = (bf16[256,1024]{1,0:T(8,128)(2,1)}, f32[1024,1024]{1,0:T(8,128)}) custom-call(bf16[256,1024]{1,0:T(8,128)(2,1)S(1)} %get-tuple-element.8.grad, f32[512,1024]{1,0:T(8,128)S(1)} %get-tuple-element.9.part, bf16[1024,1024]{1,0:T(8,128)(2,1)S(1)} %get-tuple-element.10.x_all, bf16[1024,1024]{1,0:T(8,128)(2,1)S(1)} %get-tuple-element.11.g_all), custom_call_target="tpu_custom_call" | custom-call | tf_op jit(solution)/shard_map/pallas_call | solution.py:591

commit v6 on v3

--- a/solution.py
+++ b/solution.py
@@ -15,7 +15,7 @@
 FILL, FULL = 1, 5
 DRAIN, STOP = 4, 8
 LEAD = 2
-STEPS, KEPT = 4, 2
+STEPS, KEPT = 8, 5
 LIMIT = 32
 NT = (((1,), (1,)), ((), ()))
 TN = (((0,), (0,)), ((), ()))
@@ -581,7 +581,7 @@
             dma((pairs,)), dma(()), dma((MICRO, pairs - 1)), dma((pairs,)), dma((pairs,)),
             dma((replicas,)), dma((replicas,)),
         ],
-        compiler_params=pltpu.CompilerParams(collective_id=0, has_side_effects=True, vmem_limit_bytes=57 * 2**20),
+        compiler_params=pltpu.CompilerParams(collective_id=0, has_side_effects=True, vmem_limit_bytes=57 * 2**20 - 2**18),
     )(weights[0], codes[0], scales, grad_out)
     grad_in, weight_grad = pl.pallas_call(
         closing_kernel,

time: 55 us -> 54.9 us (level)
  no operation moved by 1% of the time
where the time goes in v6:
time: 54.9 us; the launch traced here: 54.7 us
  Pallas kernels  54.1 us (99%)
  between operations  0.64 us (1%)
    pallas_call x1, Pallas kernels, per_device(): pl.pallas_call(functools.partial(relay_kernel, sections=sections, shards=...  51.9 us
    pallas_call x1, Pallas kernels, per_device(): pl.pallas_call(closing_kernel, out_shape=(jax.ShapeDtypeStruct((tok, cols...  2.22 us

profile of v6, /device:TPU:0, one launch (start us, length us, event | category | flops | bytes accessed | tf_op | source)
XLA Modules:
  0.0 54.7 jit_solution(6949981470768899233)
XLA Ops:
  0.6 51.9 %shard_map.59 = (bf16[256,1024]{1,0:T(8,128)(2,1)S(1)}, f32[640,1024]{1,0:T(8,128)S(1)}, bf16[1024,1024]{1,0:T(8,128)(2,1)S(1)}, bf16[1024,1024]{1,0:T(8,128)(2,1)S(1)}) custom-call(bf16[4096,1024]{1,0:T(8,128)(2,1)} %bitcast.4, s32[256,4096]{1,0:T(8,128)} %bitcast.5, f32[1,256]{1,0:T(1,128)} %scales.1, bf16[256,1024]{1,0:T(8,128)(2,1)} %grad_out.1), custom_call_target="tpu_custom_call" | custom-call | tf_op jit(solution)/shard_map/pallas_call | solution.py:558
  52.5 2.2 %shard_map.60 = (bf16[256,1024]{1,0:T(8,128)(2,1)}, f32[1024,1024]{1,0:T(8,128)}) custom-call(bf16[256,1024]{1,0:T(8,128)(2,1)S(1)} %get-tuple-element.8.grad, f32[640,1024]{1,0:T(8,128)S(1)} %get-tuple-element.9.part, bf16[1024,1024]{1,0:T(8,128)(2,1)S(1)} %get-tuple-element.10.x_all, bf16[1024,1024]{1,0:T(8,128)(2,1)S(1)} %get-tuple-element.11.g_all), custom_call_target="tpu_custom_call" | custom-call | tf_op jit(solution)/shard_map/pallas_call | solution.py:586
